TPU v7x, 32 devices: a whole 2x2x4 slice. The times are simulated.
32 devices in a mesh: pts: 4 (over y, x), lmk: 8 (over z, core).
Axes of the slice: x: 2, y: 2, z: 4, core: 2. Of those that a mesh axis runs over, the one named last changes fastest.
Arguments:
- points: float32 [16384, 384], P('pts'), may hold values from -8 to 8
- labels: int32 [16384], P('pts'), may hold values from 0 to 127
- landmarks: float32 [16384, 384], P('lmk'), may hold values from -8 to 8
- coefficients: float32 [16384, 128], P('lmk'), may hold values from -4 to 4
Outputs:
- gradient: float32 [16384, 128], P('lmk')
All inputs are finite; a program needn't handle non-finite values.
Results may differ from a plain program's by a relative error of at most 0.0003.
Values sent between devices are 32-bit elements; how exact they have to be, the bound alone decides.
A program may use at most 128 MiB of HBM per device.

v0:
```python
import jax
import jax.numpy as jnp
from jax import lax
from jax.sharding import PartitionSpec as P

LOSS_SCALE = 8192.0
RIDGE = 0.5


def residual_rows(logits, labels):
    classes = logits.shape[1]
    expo = jnp.exp(logits)
    onehot = (labels[:, None] == jnp.arange(classes, dtype=jnp.int32)[None, :]).astype(jnp.float32)
    return expo / jnp.sum(expo, axis=1, keepdims=True) - onehot


def per_device(points, labels, landmarks, coefficients):
    high = lax.Precision.HIGHEST
    feats = points.shape[1]
    pnorm = jnp.sum(points * points, axis=1)
    lnorm = jnp.sum(landmarks * landmarks, axis=1)
    cross = jnp.dot(points, landmarks.T, precision=high, preferred_element_type=jnp.float32)
    kernel = jnp.exp(-(pnorm[:, None] + lnorm[None, :] - 2.0 * cross) / feats)
    partial_logits = jnp.dot(
        kernel, coefficients, precision=high, preferred_element_type=jnp.float32
    )
    logits = lax.psum(partial_logits, "lmk")
    resid = residual_rows(logits, labels)
    local_terms = lax.dot_general(
        kernel, resid, (((0,), (0,)), ((), ())), precision=high, preferred_element_type=jnp.float32
    )
    summed = lax.psum(local_terms, "pts")
    total_points = labels.shape[0] * lax.axis_size("pts")
    return summed * (LOSS_SCALE / total_points) + RIDGE * coefficients


def solution(mesh):
    in_specs = (P("pts", None), P("pts"), P("lmk", None), P("lmk", None))
    out_specs = P("lmk", None)
    return jax.shard_map(
        per_device, mesh=mesh, in_specs=in_specs, out_specs=out_specs, check_vma=False
    )
```

profile of v0, /device:TPU:0, one launch (start us, length us, event | category | flops | bytes accessed | tf_op | source)
XLA Modules:
  0.0 299.8 jit_solution(14387722691670884355)
XLA Ops:
  6.5 0.0 copy-start
  6.5 0.0 all-reduce.3.cloned.1.call-start
  6.5 2.3 multiply_reduce_fusion.1
  8.9 3.4 %multiply_reduce_fusion = f32[4096]{0:T(1024)S(1)} fusion(f32[4096,384]{1,0:T(8,128)} %param.4), kind=kLoop, calls=%fused_computation.11 | loop fusion | flops 3141632 | bytes 6307840 | tf_op jit(solution)/shard_map/reduce_sum | solution.py:20
  12.3 58.6 %fusion.20 = f32[4096,2048]{1,0:T(8,128)} fusion(f32[4096,384]{1,0:T(8,128)} %param.4, f32[2048,384]{1,0:T(8,128)} %param.6), kind=kOutput, calls=%fused_computation.26 | convolution fusion | flops 38654705664 | bytes 42991616 | tf_op jit(solution)/shard_map/dot_general | solution.py:22
  70.9 0.0 copy-done
  70.9 0.0 copy-start.1
  70.9 35.0 %fusion.1 = f32[4096,128]{1,0:T(8,128)} fusion(f32[2048,128]{1,0:T(8,128)S(1)} %copy-done, f32[4096,2048]{1,0:T(8,128)} %fusion.20, f32[2048]{0:T(1024)S(1)} %multiply_reduce_fusion.1, f32[4096]{0:T(1024)S(1)} %multiply_reduce_fusion), kind=kOutput, calls=%fused_computation.2 | convolution fusion | flops 12926844928 | bytes 36724736 | tf_op jit(solution)/shard_map/dot_general | solution.py:24
  105.8 0.0 all-reduce.3.cloned.1.call-update
  105.8 0.0 all-reduce.5.cloned.1.call-start
  105.9 68.0 %all-reduce.3.cloned.1.call-done = f32[4096,128]{1,0:T(8,128)} async-done(((f32[4096,128]{1,0:T(8,128)}), f32[4096,128]{1,0:T(8,128)}) %all-reduce.3.cloned.1.call-update) | async-done | bytes 2097168 | tf_op jit(solution)/shard_map/psum | solution.py:27
  173.9 2.2 exponential_reduce_fusion
  176.1 0.0 copy-done.1
  176.1 62.3 %fusion = f32[2048,128]{1,0:T(8,128)} fusion(f32[4096,2048]{1,0:T(8,128)} %fusion.20, f32[2048]{0:T(1024)S(1)} %multiply_reduce_fusion.1, f32[4096]{0:T(1024)S(1)} %multiply_reduce_fusion, f32[4096,128]{1,0:T(8,128)} %all-reduce.3.cloned.1.call-done, s32[4096]{0:T(1024)S(1)} %copy-done.1, f32[4096]{0:T(1024)S(1)} %exponential_reduce_fusion), kind=kOutput, calls=%fused_computation.1 | convolution fusion | flops 12928942080 | bytes 36757504 | tf_op jit(solution)/shard_map/dot_general | solution.py:29
  238.4 0.0 all-reduce.5.cloned.1.call-update
  238.4 52.2 %all-reduce.5.cloned.1.call-done = f32[2048,128]{1,0:T(8,128)} async-done(((f32[2048,128]{1,0:T(8,128)}), f32[2048,128]{1,0:T(8,128)}) %all-reduce.5.cloned.1.call-update) | async-done | bytes 1048592 | tf_op jit(solution)/shard_map/psum | solution.py:32
  290.6 2.3 add_multiply_fusion
Async XLA Ops:
  6.5 64.3 %copy-start = (f32[2048,128]{1,0:T(8,128)S(1)}, f32[2048,128]{1,0:T(8,128)}, u32[]{:S(2)}) copy-start(f32[2048,128]{1,0:T(8,128)} %param.7) | copy-start | bytes 3145732
  6.5 167.4 %all-reduce.3.cloned.1.call-start = ((), (), s32[]{:S(2)}) async-start(), calls=%async_computation | async-start | bytes 4194304 | tf_op jit(solution)/shard_map/psum | solution.py:27
  70.9 105.3 %copy-start.1 = (s32[4096]{0:T(1024)S(1)}, s32[4096]{0:T(1024)}, u32[]{:S(2)}) copy-start(s32[4096]{0:T(1024)} %param.5) | copy-start | bytes 49156
  105.8 184.8 %all-reduce.5.cloned.1.call-start = ((), (), s32[]{:S(2)}) async-start(), calls=%async_computation.1 | async-start | bytes 2097152 | tf_op jit(solution)/shard_map/psum | solution.py:32
Sparse Core Ops, SparseCore 0:
  106.0 67.8 all-reduce.2
  238.5 52.0 all-reduce.4
where the time goes:
time: 300 us
  matrix products  156 us (52%)
  waiting for transfers between devices  120 us (40%)
  between operations  13.4 us (4%)
  other arithmetic  10.2 us (3%)
    psum x1, waiting for transfers between devices, per_device(): logits = lax.psum(partial_logits, 'lmk')  68 us
    dot_general x1, matrix products, per_device(): lax.dot_general(kernel, resid, (((0,), (0,)), ((), ())), precision=high,...  62.3 us
    dot_general x1, matrix products, per_device(): jnp.dot(points, landmarks.T, precision=high, preferred_element_type=jnp.f...  58.6 us
    psum x1, waiting for transfers between devices, per_device(): summed = lax.psum(local_terms, 'pts')  52.2 us
    dot_general x1, matrix products, per_device(): jnp.dot(kernel, coefficients, precision=high, preferred_element_type=jnp....  35 us
  transfers between devices with their start and end apart: 2, of which 2 were waited for; matrix products, arithmetic and copies ran while one was open for 0% of the time, Pallas kernels for 0%

commit v1 on v0

--- a/solution.py
+++ b/solution.py
@@ -29,7 +29,9 @@
     local_terms = lax.dot_general(
         kernel, resid, (((0,), (0,)), ((), ())), precision=high, preferred_element_type=jnp.float32
     )
-    summed = lax.psum(local_terms, "pts")
+    summed = local_terms
+    for hop in (1, 2):
+        summed = summed + lax.ppermute(summed, "pts", [(dev, dev ^ hop) for dev in range(4)])
     total_points = labels.shape[0] * lax.axis_size("pts")
     return summed * (LOSS_SCALE / total_points) + RIDGE * coefficients
 

time: 300 us -> 292 us (0.973)
  waiting for transfers between devices: 120 us -> 111 us
  starting transfers between devices: 0.04 us -> 3.08 us
    psum x1 -> x0, waiting for transfers between devices: 52.2 us -> none  [per_device(): summed = lax.psum(local_terms, 'pts')]
    ppermute x0 -> x2, waiting for transfers between devices: none -> 43.1 us  [per_device(): lax.ppermute(summed, 'pts', [(dev, dev ^ hop) for dev in range(4)])]
    ppermute x0 -> x2, starting transfers between devices: none -> 3.08 us  [per_device(): lax.ppermute(summed, 'pts', [(dev, dev ^ hop) for dev in range(4)])]
  transfers between devices with their start and end apart: 2 -> 3, of which waited for: 2 -> 3; matrix products, arithmetic and copies ran while one was open for 0% -> 0% of each run, Pallas kernels for 0% -> 0%
where the time goes in v1:
time: 292 us
  matrix products  155 us (53%)
  waiting for transfers between devices  111 us (38%)
  between operations  13.4 us (5%)
  other arithmetic  9.23 us (3%)
  starting transfers between devices  3.08 us (1%)
    psum x1, waiting for transfers between devices, per_device(): logits = lax.psum(partial_logits, 'lmk')  68.1 us
    dot_general x1, matrix products, per_device(): lax.dot_general(kernel, resid, (((0,), (0,)), ((), ())), precision=high,...  61.3 us
    dot_general x1, matrix products, per_device(): jnp.dot(points, landmarks.T, precision=high, preferred_element_type=jnp.f...  58.6 us
    ppermute x2, waiting for transfers between devices, per_device(): lax.ppermute(summed, 'pts', [(dev, dev ^ hop) for dev in range(4)])  43.1 us
    dot_general x1, matrix products, per_device(): jnp.dot(kernel, coefficients, precision=high, preferred_element_type=jnp....  35 us
  transfers between devices with their start and end apart: 3, of which 3 were waited for; matrix products, arithmetic and copies ran while one was open for 0% of the time, Pallas kernels for 0%

profile of v1, /device:TPU:0, one launch (start us, length us, event | category | flops | bytes accessed | tf_op | source)
XLA Modules:
  0.0 291.8 jit_solution(4223287921521084234)
XLA Ops:
  6.5 0.0 copy-start
  6.5 0.0 all-reduce.2.cloned.1.call-start
  6.5 2.3 multiply_reduce_fusion.1
  8.9 3.4 %multiply_reduce_fusion = f32[4096]{0:T(1024)S(1)} fusion(f32[4096,384]{1,0:T(8,128)} %param.4), kind=kLoop, calls=%fused_computation.11 | loop fusion | flops 3141632 | bytes 6307840 | tf_op jit(solution)/shard_map/reduce_sum | solution.py:20
  12.3 58.6 %fusion.20 = f32[4096,2048]{1,0:T(8,128)} fusion(f32[4096,384]{1,0:T(8,128)} %param.4, f32[2048,384]{1,0:T(8,128)} %param.6), kind=kOutput, calls=%fused_computation.26 | convolution fusion | flops 38654705664 | bytes 42991616 | tf_op jit(solution)/shard_map/dot_general | solution.py:22
  70.9 0.0 copy-done
  70.9 0.0 copy-start.1
  70.9 35.0 %fusion.1 = f32[4096,128]{1,0:T(8,128)} fusion(f32[2048,128]{1,0:T(8,128)S(1)} %copy-done, f32[4096,2048]{1,0:T(8,128)} %fusion.20, f32[2048]{0:T(1024)S(1)} %multiply_reduce_fusion.1, f32[4096]{0:T(1024)S(1)} %multiply_reduce_fusion), kind=kOutput, calls=%fused_computation.2 | convolution fusion | flops 12926844928 | bytes 36724736 | tf_op jit(solution)/shard_map/dot_general | solution.py:24
  105.8 0.0 all-reduce.2.cloned.1.call-update
  105.8 68.1 %all-reduce.2.cloned.1.call-done = f32[4096,128]{1,0:T(8,128)} async-done(((f32[4096,128]{1,0:T(8,128)}), f32[4096,128]{1,0:T(8,128)}) %all-reduce.2.cloned.1.call-update) | async-done | bytes 2097168 | tf_op jit(solution)/shard_map/psum | solution.py:27
  173.9 2.2 exponential_reduce_fusion
  176.1 0.0 copy-done.1
  176.1 61.3 %fusion = f32[2048,128]{1,0:T(8,128)S(1)} fusion(f32[4096,2048]{1,0:T(8,128)} %fusion.20, f32[2048]{0:T(1024)S(1)} %multiply_reduce_fusion.1, f32[4096]{0:T(1024)S(1)} %multiply_reduce_fusion, f32[4096,128]{1,0:T(8,128)} %all-reduce.2.cloned.1.call-done, s32[4096]{0:T(1024)S(1)} %copy-done.1, f32[4096]{0:T(1024)S(1)} %exponential_reduce_fusion), kind=kOutput, calls=%fused_computation.1 | convolution fusion | flops 12928942080 | bytes 36757504 | tf_op jit(solution)/shard_map/dot_general | solution.py:29
  237.4 1.5 collective-permute-start
  239.0 22.0 %collective-permute-done = f32[2048,128]{1,0:T(8,128)S(1)} collective-permute-done((f32[2048,128]{1,0:T(8,128)S(1)}, f32[2048,128]{1,0:T(8,128)S(1)}, u32[]{:S(2)}, u32[]{:S(2)}) %collective-permute-start) | collective-permute-done | bytes 1048608 | tf_op jit(solution)/shard_map/ppermute | solution.py:34
  261.0 0.1 add.28
  261.1 1.5 collective-permute-start.1
  262.6 21.1 %collective-permute-done.1 = f32[2048,128]{1,0:T(8,128)S(1)} collective-permute-done((f32[2048,128]{1,0:T(8,128)S(1)}, f32[2048,128]{1,0:T(8,128)S(1)}, u32[]{:S(2)}, u32[]{:S(2)}) %collective-permute-start.1) | collective-permute-done | bytes 1048608 | tf_op jit(solution)/shard_map/ppermute | solution.py:34
  283.7 1.2 add_multiply_fusion
Async XLA Ops:
  6.5 64.3 %copy-start = (f32[2048,128]{1,0:T(8,128)S(1)}, f32[2048,128]{1,0:T(8,128)}, u32[]{:S(2)}) copy-start(f32[2048,128]{1,0:T(8,128)} %param.7) | copy-start | bytes 3145732
  6.5 167.4 %all-reduce.2.cloned.1.call-start = ((), (), s32[]{:S(2)}) async-start(), calls=%async_computation | async-start | bytes 4194304 | tf_op jit(solution)/shard_map/psum | solution.py:27
  70.9 105.3 %copy-start.1 = (s32[4096]{0:T(1024)S(1)}, s32[4096]{0:T(1024)}, u32[]{:S(2)}) copy-start(s32[4096]{0:T(1024)} %param.5) | copy-start | bytes 49156
  237.4 23.5 %collective-permute-start = (f32[2048,128]{1,0:T(8,128)S(1)}, f32[2048,128]{1,0:T(8,128)S(1)}, u32[]{:S(2)}, u32[]{:S(2)}) collective-permute-start(f32[2048,128]{1,0:T(8,128)S(1)} %fusion), channel_id=1, source_target_pairs={{0,8},{8,0},{16,24},{24,16},{1,9},{9,1},{17,25},{25,17},{2,10},{10... | collective-permute-start | bytes 3145736 | tf_op jit(solution)/shard_map/ppermute | solution.py:34
  261.1 22.7 %collective-permute-start.1 = (f32[2048,128]{1,0:T(8,128)S(1)}, f32[2048,128]{1,0:T(8,128)S(1)}, u32[]{:S(2)}, u32[]{:S(2)}) collective-permute-start(f32[2048,128]{1,0:T(8,128)S(1)} %add.28), channel_id=1, source_target_pairs={{0,16},{8,24},{16,0},{24,8},{1,17},{9,25},{17,1},{25,9},{2,18},{10... | collective-permute-start | bytes 3145736 | tf_op jit(solution)/shard_map/ppermute | solution.py:34
Sparse Core Ops, SparseCore 0:
  106.0 67.8 all-reduce.1
